TPU v7x, 256 devices: a whole 4x4x8 slice. The times are simulated.
256 devices in a mesh: fsdp: 32 (over z_hi, x, y), ep: 8 (over z_lo, core).
Axes of the slice: x: 4, y: 4, z: 8 (z_hi: 2, z_lo: 4; z = z_hi * 4 + z_lo), core: 2. Of those that a mesh axis runs over, the one named last changes fastest.
Arguments:
- tokens: bfloat16 [32768, 2048], P(('fsdp', 'ep')), may hold values from -24 to 24
- routes: int32 [32768, 6], P(('fsdp', 'ep')), may hold values from 0 to 63, as said below
- route_weight: float32 [32768, 6], P(('fsdp', 'ep')), may hold values from 0.1 to 1
- w_in: bfloat16 [8, 2048, 2, 768], P('ep', 'fsdp'), may hold values from -0.125 to 0.125
- w_down: bfloat16 [8, 768, 2048], P('ep', 'fsdp'), may hold values from -0.21875 to 0.21875
- cotangent: bfloat16 [32768, 2048], P(('fsdp', 'ep')), may hold values from -6 to 6
Outputs:
- layer_out: bfloat16 [32768, 2048], P(('fsdp', 'ep'))
- grad_tokens: bfloat16 [32768, 2048], P(('fsdp', 'ep'))
- grad_in: float32 [8, 2048, 2, 768], P('ep', 'fsdp')
- grad_down: float32 [8, 768, 2048], P('ep', 'fsdp')
Inputs may be any that keep to these rules, and one draw needn't show every extreme that they name: `routes`: each row names 6 different experts. The rows of one device name each window expert 0 to 7 at most 32 times; in every draw every device names some window expert exactly 32 times, and for some index of fsdp one window expert is named exactly 32 times by each device with that index.
All inputs are finite; a program needn't handle non-finite values.
Results may differ from a plain program's by a relative error of at most 0.014.
Values may be sent and summed in bfloat16 or wider, within the bound.
A program may use at most 64 MiB of HBM per device.

v0:
```python
import jax
import jax.numpy as jnp
from jax import lax
from jax.sharding import PartitionSpec as P

D = 2048
FF = 768
CAP = 32


def contract_rows(left, right):
    return lax.dot_general(
        left, right, (((0,), (0,)), ((), ())), preferred_element_type=jnp.float32
    )


def contract_cols(left, right):
    return lax.dot_general(
        left, right, (((1,), (1,)), ((), ())), preferred_element_type=jnp.float32
    )


def local(tokens, routes, route_weight, w_in, w_down, cotangent):
    ep_width = lax.axis_size("ep")
    all_rows = ep_width * CAP
    expert_ids = jnp.arange(ep_width, dtype=jnp.int32)
    route_hits = routes[:, :, None] == expert_ids[None, None, :]
    member = jnp.any(route_hits, axis=1).astype(jnp.int32)
    route_coef = jnp.sum(jnp.where(route_hits, route_weight[:, :, None], 0.0), axis=1)
    slot_rank = jnp.cumsum(member, axis=0) - member
    slot_ids = jnp.arange(CAP, dtype=jnp.int32)
    slot_hits = (slot_rank.T[:, None, :] == slot_ids[None, :, None]) & (member.T[:, None, :] > 0)
    dispatch = slot_hits.astype(jnp.bfloat16)
    slot_coef = jnp.sum(jnp.where(slot_hits, route_coef.T[:, None, :], 0.0), axis=2)
    weighted_dispatch = jnp.where(slot_hits, route_coef.T[:, None, :], 0.0)
    send_x = jnp.einsum("est,td->esd", dispatch, tokens, preferred_element_type=jnp.float32).astype(
        jnp.bfloat16
    )
    dy_rows = jnp.einsum("est,td->esd", dispatch, cotangent, preferred_element_type=jnp.float32)
    send_dy = (dy_rows * slot_coef[:, :, None]).astype(jnp.bfloat16)
    full_in, full_down = (
        lax.all_gather(w_in[0], "fsdp", axis=0, tiled=True),
        lax.all_gather(w_down[0], "fsdp", axis=0, tiled=True),
    )
    flat_in = full_in.reshape(D, 2 * FF)
    recv_x = lax.all_to_all(send_x, "ep", split_axis=0, concat_axis=0, tiled=True)
    rows_x = recv_x.reshape(all_rows, D)
    gate_up = jnp.dot(rows_x, flat_in, preferred_element_type=jnp.float32)
    gate_vals = gate_up[:, :FF]
    up_vals = gate_up[:, FF:]
    sig_gate = jax.nn.sigmoid(gate_vals)
    act_vals = gate_vals * sig_gate
    hidden = (act_vals * up_vals).astype(jnp.bfloat16)
    out_rows = jnp.dot(hidden, full_down, preferred_element_type=jnp.float32).astype(jnp.bfloat16)
    out_rows = out_rows.reshape(ep_width, CAP, D)
    back_out = lax.all_to_all(out_rows, "ep", split_axis=0, concat_axis=0, tiled=True)
    recv_dy = lax.all_to_all(send_dy, "ep", split_axis=0, concat_axis=0, tiled=True)
    rows_dy = recv_dy.reshape(all_rows, D)
    grad_hidden = contract_cols(rows_dy, full_down)
    grad_gate = grad_hidden * up_vals * sig_gate * (1.0 + gate_vals * (1.0 - sig_gate))
    grad_up = grad_hidden * act_vals
    grad_gu = jnp.concatenate([grad_gate, grad_up], axis=1).astype(jnp.bfloat16)
    input_rows = contract_cols(grad_gu, flat_in).astype(jnp.bfloat16).reshape(ep_width, CAP, D)
    term_in = contract_rows(rows_x, grad_gu)
    term_down = contract_rows(hidden, rows_dy)
    grad_in, grad_down = (
        lax.psum_scatter(
            term_in.astype(jnp.bfloat16), "fsdp", scatter_dimension=0, tiled=True
        ).astype(jnp.float32),
        lax.psum_scatter(
            term_down.astype(jnp.bfloat16), "fsdp", scatter_dimension=0, tiled=True
        ).astype(jnp.float32),
    )
    back_dx = lax.all_to_all(input_rows, "ep", split_axis=0, concat_axis=0, tiled=True)
    mixed_sum = jnp.einsum(
        "est,esd->td",
        weighted_dispatch,
        back_out.astype(jnp.float32),
        preferred_element_type=jnp.float32,
    )
    grad_sum = jnp.einsum("est,esd->td", dispatch, back_dx, preferred_element_type=jnp.float32)
    layer_out = mixed_sum.astype(jnp.bfloat16)
    grad_tokens = grad_sum.astype(jnp.bfloat16)
    grad_in = grad_in.reshape(w_in.shape)
    grad_down = grad_down.reshape(w_down.shape)
    return (layer_out, grad_tokens, grad_in, grad_down)


def solution(mesh):
    in_specs = (
        P(("fsdp", "ep"), None),
        P(("fsdp", "ep"), None),
        P(("fsdp", "ep"), None),
        P("ep", "fsdp", None, None),
        P("ep", "fsdp", None),
        P(("fsdp", "ep"), None),
    )
    out_specs = (
        P(("fsdp", "ep"), None),
        P(("fsdp", "ep"), None),
        P("ep", "fsdp", None, None),
        P("ep", "fsdp", None),
    )
    return jax.shard_map(local, mesh=mesh, in_specs=in_specs, out_specs=out_specs, check_vma=False)
```

profile of v0, /device:TPU:1, one launch (start us, length us, event | category | flops | bytes accessed | tf_op | source)
XLA Modules:
  0.0 798.5 jit_solution(17378542734916853659)
XLA Ops:
  7.2 0.0 copy-start
  7.2 0.0 copy-start.4
  7.2 0.0 copy-start.5
  7.2 0.0 copy-start.2
  7.2 0.0 all-gather.5.cloned.1.call-start
  7.3 0.7 all-gather.5.cloned.1.call-update
  7.9 0.0 all-gather.7.cloned.1.call-start
  8.0 0.7 all-gather.7.cloned.1.call-update
  8.7 0.7 fusion.29
  9.4 0.1 copy.19
  9.5 0.1 copy.21
  9.6 0.2 reduce_window_sum.11
  9.9 0.0 copy-done
  9.9 1.5 convolution_convert_fusion.2
  11.3 7.4 all-to-all-start
  18.7 0.0 copy-done.4
  18.7 0.0 copy-done.5
  18.7 0.1 select_reduce_fusion
  18.8 0.0 copy-done.2
  18.9 1.5 fusion.4
  20.4 26.9 %all-to-all-done = bf16[8,32,2048]{2,1,0:T(8,128)(2,1)S(1)} async-done(((bf16[8,32,2048]{2,1,0:T(8,128)(2,1)}), bf16[8,32,2048]{2,1,0:T(8,128)(2,1)S(1)}, u32[]{:S(2)}, u32[]{:S(2)}) %all-to-all-start) | async-done | bytes 1048608 | tf_op jit(solution)/shard_map/all_to_all | solution.py:46
  47.2 4.3 all-to-all-start.2
  51.6 0.0 reduce-scatter.5.cloned.1.call-start
  51.6 108.5 %all-gather.5.cloned.1.call-done = bf16[1,2048,2,768]{3,2,0,1:T(2,128)(2,1)} async-done(((bf16[1,64,2,768]{3,2,0,1:T(2,128)(2,1)}), bf16[1,2048,2,768]{3,2,0,1:T(2,128)(2,1)}) %all-gather.5.cloned.1.call-update) | async-done | bytes 6291472 | tf_op jit(solution)/shard_map/all_gather | solution.py:42
  160.1 4.1 copy.23
  164.2 0.0 copy-start.1
  164.2 2.7 copy-done.1
  166.9 2.9 fusion.33
  169.8 0.0 all-to-all-done.2
  169.8 88.4 %all-gather.7.cloned.1.call-done = bf16[1,768,2048]{2,1,0:T(8,128)(2,1)} async-done(((bf16[1,24,2048]{2,1,0:T(8,128)(2,1)}), bf16[1,768,2048]{2,1,0:T(8,128)(2,1)}) %all-gather.7.cloned.1.call-update) | async-done | bytes 3145744 | tf_op jit(solution)/shard_map/all_gather | solution.py:43
  258.2 4.3 multiply_convert_fusion.1
  262.5 2.7 convolution_convert_fusion.1
  265.2 0.0 copy-start.3
  265.2 0.0 reduce-scatter.5.cloned.1.call-update
  265.2 0.0 reduce-scatter.3.cloned.1.call-start
  265.3 0.9 copy-done.3
  266.2 4.5 convolution_convert_fusion
  270.7 0.0 reduce-scatter.3.cloned.1.call-update
  270.7 3.9 fusion.5
  274.6 5.8 all-to-all-start.1
  280.4 5.7 convolution_convert_fusion.3
  286.0 22.8 %all-to-all-done.1 = bf16[8,32,2048]{2,1,0:T(8,128)(2,1)S(1)} async-done(((bf16[8,32,2048]{2,1,0:T(8,128)(2,1)}), bf16[8,32,2048]{2,1,0:T(8,128)(2,1)S(1)}, u32[]{:S(2)}, u32[]{:S(2)}) %all-to-all-start.1) | async-done | bytes 1048608 | tf_op jit(solution)/shard_map/all_to_all | solution.py:56
  308.8 4.3 all-to-all-start.3
  313.2 1.1 fusion.8
  314.3 27.2 %all-to-all-done.3 = bf16[8,32,2048]{2,1,0:T(8,128)(2,1)S(1)} async-done(((bf16[8,32,2048]{2,1,0:T(8,128)(2,1)}), bf16[8,32,2048]{2,1,0:T(8,128)(2,1)S(1)}, u32[]{:S(2)}, u32[]{:S(2)}) %all-to-all-start.3) | async-done | bytes 1048608 | tf_op jit(solution)/shard_map/all_to_all | solution.py:74
  341.5 1.1 fusion.9
  342.7 176.0 %reduce-scatter.5.cloned.1.call-done = bf16[24,2048]{1,0:T(8,128)(2,1)} async-done(((bf16[768,2048]{1,0:T(8,128)(2,1)}), bf16[24,2048]{1,0:T(8,128)(2,1)}) %reduce-scatter.5.cloned.1.call-update) | async-done | bytes 98320 | tf_op jit(solution)/shard_map/reduce_scatter | solution.py:70
  518.7 1.6 bitcast_convert_fusion
  520.3 269.7 %reduce-scatter.3.cloned.1.call-done = bf16[64,1536]{1,0:T(8,128)(2,1)} async-done(((bf16[2048,1536]{1,0:T(8,128)(2,1)}), bf16[64,1536]{1,0:T(8,128)(2,1)}) %reduce-scatter.3.cloned.1.call-update) | async-done | bytes 196624 | tf_op jit(solution)/shard_map/reduce_scatter | solution.py:67
  790.0 1.9 reshape.52
  (4 shorter events, 0.1 us)
Async XLA Ops:
  7.2 2.7 copy-start
  7.2 11.5 %copy-start.4 = (s32[128,6]{0,1:T(8,128)S(1)}, s32[128,6]{0,1:T(8,128)}, u32[]{:S(2)}) copy-start(s32[128,6]{0,1:T(8,128)} %param.7) | copy-start | bytes 9220
  7.2 11.5 %copy-start.5 = (f32[128,6]{0,1:T(8,128)S(1)}, f32[128,6]{0,1:T(8,128)}, u32[]{:S(2)}) copy-start(f32[128,6]{0,1:T(8,128)} %param.8) | copy-start | bytes 9220
  7.2 11.6 %copy-start.2 = (bf16[128,2048]{1,0:T(8,128)(2,1)S(1)}, bf16[128,2048]{1,0:T(8,128)(2,1)}, u32[]{:S(2)}) copy-start(bf16[128,2048]{1,0:T(8,128)(2,1)} %param.11) | copy-start | bytes 1572868
  7.2 152.9 %all-gather.5.cloned.1.call-start = ((), (), s32[]{:S(2)}) async-start(), calls=%async_computation.8 | async-start | bytes 6488064 | tf_op jit(solution)/shard_map/all_gather | solution.py:42
  7.9 250.3 %all-gather.7.cloned.1.call-start = ((), (), s32[]{:S(2)}) async-start(), calls=%async_computation.9 | async-start | bytes 3244032 | tf_op jit(solution)/shard_map/all_gather | solution.py:43
  11.3 35.9 %all-to-all-start = ((bf16[8,32,2048]{2,1,0:T(8,128)(2,1)}), bf16[8,32,2048]{2,1,0:T(8,128)(2,1)S(1)}, u32[]{:S(2)}, u32[]{:S(2)}) async-start(bf16[8,32,2048]{2,1,0:T(8,128)(2,1)} %convolution_convert_fusion.2), calls=%async_computation | async-start | bytes 2097152 | tf_op jit(solution)/shard_map/all_to_all | solution.py:46
  47.2 122.6 %all-to-all-start.2 = ((bf16[8,32,2048]{2,1,0:T(8,128)(2,1)}), bf16[8,32,2048]{2,1,0:T(8,128)(2,1)S(1)}, u32[]{:S(2)}, u32[]{:S(2)}) async-start(bf16[8,32,2048]{2,1,0:T(8,128)(2,1)} %fusion.4), calls=%async_computation.2 | async-start | bytes 2097152 | tf_op jit(solution)/shard_map/all_to_all | solution.py:57
  51.6 467.1 %reduce-scatter.5.cloned.1.call-start = ((), (), s32[]{:S(2)}) async-start(), calls=%async_computation.7 | async-start | bytes 3244032 | tf_op jit(solution)/shard_map/reduce_scatter | solution.py:70
  164.2 2.7 copy-start.1
  265.2 1.0 copy-start.3
  265.2 524.8 %reduce-scatter.3.cloned.1.call-start = ((), (), s32[]{:S(2)}) async-start(), calls=%async_computation.6 | async-start | bytes 6488064 | tf_op jit(solution)/shard_map/reduce_scatter | solution.py:67
  274.6 34.2 %all-to-all-start.1 = ((bf16[8,32,2048]{2,1,0:T(8,128)(2,1)}), bf16[8,32,2048]{2,1,0:T(8,128)(2,1)S(1)}, u32[]{:S(2)}, u32[]{:S(2)}) async-start(bf16[8,32,2048]{2,1,0:T(8,128)(2,1)} %bitcast.7), calls=%async_computation.1 | async-start | bytes 2097152 | tf_op jit(solution)/shard_map/all_to_all | solution.py:56
  308.8 32.7 %all-to-all-start.3 = ((bf16[8,32,2048]{2,1,0:T(8,128)(2,1)}), bf16[8,32,2048]{2,1,0:T(8,128)(2,1)S(1)}, u32[]{:S(2)}, u32[]{:S(2)}) async-start(bf16[8,32,2048]{2,1,0:T(8,128)(2,1)} %bitcast.57), calls=%async_computation.3 | async-start | bytes 2097152 | tf_op jit(solution)/shard_map/all_to_all | solution.py:74
Sparse Core Ops, SparseCore 0:
  11.4 148.5 all-gather.4
  163.5 94.6 all-gather.6
  265.3 253.3 reduce-scatter.4
  525.0 264.9 reduce-scatter.2
where the time goes:
time: 799 us; the launch traced here: 798 us
  waiting for transfers between devices  721 us (90%)
  matrix products  29.2 us (4%)
  starting transfers between devices  22 us (3%)
  between operations  13.8 us (2%)
  local copies, waits for them, and re-layouts  9.89 us (1%)
    reduce_scatter x1, waiting for transfers between devices, local(): lax.psum_scatter(term_in.astype(jnp.bfloat16), 'fsdp', scatter_dimension=...  270 us
    reduce_scatter x1, waiting for transfers between devices, local(): lax.psum_scatter(term_down.astype(jnp.bfloat16), 'fsdp', scatter_dimensio...  176 us
    all_gather x1, waiting for transfers between devices, local(): lax.all_gather(w_in[0], 'fsdp', axis=0, tiled=True)  108 us
    all_gather x1, waiting for transfers between devices, local(): lax.all_gather(w_down[0], 'fsdp', axis=0, tiled=True)  88.4 us
    all_to_all x1, waiting for transfers between devices, local(): lax.all_to_all(input_rows, 'ep', split_axis=0, concat_axis=0, tiled=True)  27.2 us
    all_to_all x1, waiting for transfers between devices, local(): lax.all_to_all(send_x, 'ep', split_axis=0, concat_axis=0, tiled=True)  26.9 us
    all_to_all x1, waiting for transfers between devices, local(): lax.all_to_all(out_rows, 'ep', split_axis=0, concat_axis=0, tiled=True)  22.8 us
  transfers between devices with their start and end apart: 8, of which 7 were waited for; matrix products, arithmetic and copies ran while one was open for 4% of the time, Pallas kernels for 0%

commit v1 on v0

--- a/solution.py
+++ b/solution.py
@@ -40,7 +40,9 @@
     send_dy = (dy_rows * slot_coef[:, :, None]).astype(jnp.bfloat16)
     full_in, full_down = (
         lax.all_gather(w_in[0], "fsdp", axis=0, tiled=True),
-        lax.all_gather(w_down[0], "fsdp", axis=0, tiled=True),
+        jnp.concatenate(
+            lax.all_to_all(jnp.stack([w_down[0]] * lax.axis_size("fsdp")), "fsdp", 0, 0), axis=0
+        ),
     )
     flat_in = full_in.reshape(D, 2 * FF)
     recv_x = lax.all_to_all(send_x, "ep", split_axis=0, concat_axis=0, tiled=True)

time: 799 us -> 770 us (0.964)
  waiting for transfers between devices: 721 us -> 636 us
  blocking collectives: 0 us -> 40.1 us
  starting transfers between devices: 22 us -> 36.3 us
    all_gather x1 -> x0, waiting for transfers between devices: 88.4 us -> none  [local(): lax.all_gather(w_down[0], 'fsdp', axis=0, tiled=True)]
    all_to_all x0 -> x1, blocking collectives: none -> 40.1 us  [local(): lax.all_to_all(send_x, 'ep', split_axis=0, concat_axis=0, tiled=True)]
    all_to_all x1, waiting for transfers between devices: 0.01 us -> 28.2 us  [local(): lax.all_to_all(send_dy, 'ep', split_axis=0, concat_axis=0, tiled=True)]
    all_gather x1, waiting for transfers between devices: 108 us -> 84.8 us  [local(): lax.all_gather(w_in[0], 'fsdp', axis=0, tiled=True)]
  transfers between devices with their start and end apart: 8 -> 7, of which waited for: 7 -> 7; matrix products, arithmetic and copies ran while one was open for 4% -> 4% of each run, Pallas kernels for 0% -> 0%
where the time goes in v1:
time: 770 us
  waiting for transfers between devices  636 us (83%)
  blocking collectives  40.1 us (5%)
  starting transfers between devices  36.3 us (5%)
  matrix products  28.8 us (4%)
  between operations  13.8 us (2%)
  local copies, waits for them, and re-layouts  11 us (1%)
    reduce_scatter x1, waiting for transfers between devices, local(): lax.psum_scatter(term_in.astype(jnp.bfloat16), 'fsdp', scatter_dimension=...  270 us
    reduce_scatter x1, waiting for transfers between devices, local(): lax.psum_scatter(term_down.astype(jnp.bfloat16), 'fsdp', scatter_dimensio...  182 us
    all_gather x1, waiting for transfers between devices, local(): lax.all_gather(w_in[0], 'fsdp', axis=0, tiled=True)  84.8 us
    all_to_all x1, blocking collectives, local(): lax.all_to_all(send_x, 'ep', split_axis=0, concat_axis=0, tiled=True)  40.1 us
    all_to_all x1, waiting for transfers between devices, local(): lax.all_to_all(send_dy, 'ep', split_axis=0, concat_axis=0, tiled=True)  28.2 us
    all_to_all x1, waiting for transfers between devices, local(): lax.all_to_all(input_rows, 'ep', split_axis=0, concat_axis=0, tiled=True)  27.9 us
    all_to_all x1, waiting for transfers between devices, local(): lax.all_to_all(out_rows, 'ep', split_axis=0, concat_axis=0, tiled=True)  22.5 us
    all_to_all x1, waiting for transfers between devices, local(): lax.all_to_all(jnp.stack([w_down[0]] * lax.axis_size('fsdp')), 'fsdp', 0, 0)  20.3 us
  transfers between devices with their start and end apart: 7, of which 7 were waited for; matrix products, arithmetic and copies ran while one was open for 4% of the time, Pallas kernels for 0%

profile of v1, /device:TPU:1, one launch (start us, length us, event | category | flops | bytes accessed | tf_op | source)
XLA Modules:
  0.0 769.5 jit_solution(8842844460601253918)
XLA Ops:
  7.2 0.0 copy-start
  7.2 0.0 copy-start.2
  7.2 0.0 all-gather.3.cloned.1.call-start
  7.2 0.7 all-gather.3.cloned.1.call-update
  7.9 0.7 fusion.22
  8.6 0.1 copy.19
  8.8 0.1 copy.21
  8.8 0.2 reduce_window_sum.11
  9.1 0.7 select_reduce_fusion.1
  9.8 0.1 select_reduce_fusion
  9.9 0.0 copy-done
  9.9 1.4 fusion
  11.4 0.0 copy-start.3
  11.4 7.5 all-to-all-start.3
  18.9 0.0 copy-done.2
  18.9 0.4 convolution_convert_fusion.2
  19.3 28.2 %all-to-all-done.3 = bf16[8,32,2048]{2,1,0:T(8,128)(2,1)} async-done(((bf16[8,32,2048]{2,1,0:T(8,128)(2,1)}), bf16[8,32,2048]{2,1,0:T(8,128)(2,1)}, u32[]{:S(2)}, u32[]{:S(2)}) %all-to-all-start.3) | async-done | bytes 1048608 | tf_op jit(solution)/shard_map/all_to_all | solution.py:59
  47.5 40.1 %all_to_all.25 = bf16[8,32,2048]{2,1,0:T(8,128)(2,1)S(1)} all-to-all(bf16[8,32,2048]{2,1,0:T(8,128)(2,1)S(1)} %convolution_convert_fusion.2), channel_id=1, replica_groups=mesh['fsdp'=32,'ep'=8] {'ep'}, dimensions={0} | all-to-all | bytes 2097152 | tf_op jit(solution)/shard_map/all_to_all | solution.py:48
  87.6 0.0 copy-done.3
  87.6 2.1 stack.3
  89.7 12.0 %all-to-all-start.1 = ((bf16[32,24,2048]{2,1,0:T(8,128)(2,1)}), bf16[32,24,2048]{2,1,0:T(8,128)(2,1)}, u32[]{:S(2)}, u32[]{:S(2)}) async-start(bf16[32,24,2048]{2,1,0:T(8,128)(2,1)} %stack.3), calls=%async_computation.1 | async-start | bytes 6291456 | tf_op jit(solution)/shard_map/all_to_all | solution.py:44
  101.7 0.0 reduce-scatter.5.cloned.1.call-start
  101.8 84.8 %all-gather.3.cloned.1.call-done = bf16[1,2048,2,768]{3,2,0,1:T(2,128)(2,1)} async-done(((bf16[1,64,2,768]{3,2,0,1:T(2,128)(2,1)}), bf16[1,2048,2,768]{3,2,0,1:T(2,128)(2,1)}) %all-gather.3.cloned.1.call-update) | async-done | bytes 6291472 | tf_op jit(solution)/shard_map/all_gather | solution.py:42
  186.6 4.1 copy.23
  190.7 0.0 copy-start.1
  190.8 2.6 copy-done.1
  193.4 2.9 fusion.26
  196.3 20.3 %all-to-all-done.1 = bf16[32,24,2048]{2,1,0:T(8,128)(2,1)} async-done(((bf16[32,24,2048]{2,1,0:T(8,128)(2,1)}), bf16[32,24,2048]{2,1,0:T(8,128)(2,1)}, u32[]{:S(2)}, u32[]{:S(2)}) %all-to-all-start.1) | async-done | bytes 3145760 | tf_op jit(solution)/shard_map/all_to_all | solution.py:44
  216.6 3.9 multiply_convert_fusion.1
  220.5 3.9 convolution_convert_fusion.1
  224.4 0.0 reduce-scatter.5.cloned.1.call-update
  224.4 0.0 reduce-scatter.3.cloned.1.call-start
  224.5 4.5 convolution_convert_fusion
  228.9 0.0 reduce-scatter.3.cloned.1.call-update
  229.0 3.9 convolution_convert_fusion.4
  232.8 12.2 %all-to-all-start.2 = ((bf16[8,32,2048]{2,1,0:T(8,128)(2,1)}), bf16[8,32,2048]{2,1,0:T(8,128)(2,1)S(1)}, u32[]{:S(2)}, u32[]{:S(2)}) async-start(bf16[8,32,2048]{2,1,0:T(8,128)(2,1)} %bitcast.8), calls=%async_computation.2 | async-start | bytes 2097152 | tf_op jit(solution)/shard_map/all_to_all | solution.py:58
  245.0 5.6 convolution_convert_fusion.3
  250.6 22.5 %all-to-all-done.2 = bf16[8,32,2048]{2,1,0:T(8,128)(2,1)S(1)} async-done(((bf16[8,32,2048]{2,1,0:T(8,128)(2,1)}), bf16[8,32,2048]{2,1,0:T(8,128)(2,1)S(1)}, u32[]{:S(2)}, u32[]{:S(2)}) %all-to-all-start.2) | async-done | bytes 1048608 | tf_op jit(solution)/shard_map/all_to_all | solution.py:58
  273.2 4.5 all-to-all-start.4
  277.6 1.1 fusion.1
  278.8 27.9 %all-to-all-done.4 = bf16[8,32,2048]{2,1,0:T(8,128)(2,1)S(1)} async-done(((bf16[8,32,2048]{2,1,0:T(8,128)(2,1)}), bf16[8,32,2048]{2,1,0:T(8,128)(2,1)S(1)}, u32[]{:S(2)}, u32[]{:S(2)}) %all-to-all-start.4) | async-done | bytes 1048608 | tf_op jit(solution)/shard_map/all_to_all | solution.py:76
  306.6 1.1 fusion.2
  307.8 182.1 %reduce-scatter.5.cloned.1.call-done = bf16[24,2048]{1,0:T(8,128)(2,1)} async-done(((bf16[768,2048]{1,0:T(8,128)(2,1)}), bf16[24,2048]{1,0:T(8,128)(2,1)}) %reduce-scatter.5.cloned.1.call-update) | async-done | bytes 98320 | tf_op jit(solution)/shard_map/reduce_scatter | solution.py:72
  489.9 1.6 bitcast_convert_fusion
  491.5 269.6 %reduce-scatter.3.cloned.1.call-done = bf16[64,1536]{1,0:T(8,128)(2,1)} async-done(((bf16[2048,1536]{1,0:T(8,128)(2,1)}), bf16[64,1536]{1,0:T(8,128)(2,1)}) %reduce-scatter.3.cloned.1.call-update) | async-done | bytes 196624 | tf_op jit(solution)/shard_map/reduce_scatter | solution.py:69
  761.1 1.9 reshape.57
  (3 shorter events, 0.1 us)
Async XLA Ops:
  7.2 2.8 copy-start
  7.2 11.7 %copy-start.2 = (bf16[128,2048]{1,0:T(8,128)(2,1)S(1)}, bf16[128,2048]{1,0:T(8,128)(2,1)}, u32[]{:S(2)}) copy-start(bf16[128,2048]{1,0:T(8,128)(2,1)} %param.6) | copy-start | bytes 1572868
  7.2 179.4 %all-gather.3.cloned.1.call-start = ((), (), s32[]{:S(2)}) async-start(), calls=%async_computation.9 | async-start | bytes 6488064 | tf_op jit(solution)/shard_map/all_gather | solution.py:42
  11.4 76.2 %copy-start.3 = (bf16[1,24,2048]{2,1,0:T(8,128)(2,1)S(1)}, bf16[1,24,2048]{2,1,0:T(8,128)(2,1)}, u32[]{:S(2)}) copy-start(bf16[1,24,2048]{2,1,0:T(8,128)(2,1)} %param.10) | copy-start | bytes 294916
  11.4 36.2 %all-to-all-start.3 = ((bf16[8,32,2048]{2,1,0:T(8,128)(2,1)}), bf16[8,32,2048]{2,1,0:T(8,128)(2,1)}, u32[]{:S(2)}, u32[]{:S(2)}) async-start(bf16[8,32,2048]{2,1,0:T(8,128)(2,1)} %fusion), calls=%async_computation.3 | async-start | bytes 2097152 | tf_op jit(solution)/shard_map/all_to_all | solution.py:59
  89.7 126.9 %all-to-all-start.1 = ((bf16[32,24,2048]{2,1,0:T(8,128)(2,1)}), bf16[32,24,2048]{2,1,0:T(8,128)(2,1)}, u32[]{:S(2)}, u32[]{:S(2)}) async-start(bf16[32,24,2048]{2,1,0:T(8,128)(2,1)} %stack.3), calls=%async_computation.1 | async-start | bytes 6291456 | tf_op jit(solution)/shard_map/all_to_all | solution.py:44
  101.7 388.2 %reduce-scatter.5.cloned.1.call-start = ((), (), s32[]{:S(2)}) async-start(), calls=%async_computation.8 | async-start | bytes 3244032 | tf_op jit(solution)/shard_map/reduce_scatter | solution.py:72
  190.7 2.6 copy-start.1
  224.4 536.7 %reduce-scatter.3.cloned.1.call-start = ((), (), s32[]{:S(2)}) async-start(), calls=%async_computation.7 | async-start | bytes 6488064 | tf_op jit(solution)/shard_map/reduce_scatter | solution.py:69
  232.8 40.3 %all-to-all-start.2 = ((bf16[8,32,2048]{2,1,0:T(8,128)(2,1)}), bf16[8,32,2048]{2,1,0:T(8,128)(2,1)S(1)}, u32[]{:S(2)}, u32[]{:S(2)}) async-start(bf16[8,32,2048]{2,1,0:T(8,128)(2,1)} %bitcast.8), calls=%async_computation.2 | async-start | bytes 2097152 | tf_op jit(solution)/shard_map/all_to_all | solution.py:58
  273.2 33.5 %all-to-all-start.4 = ((bf16[8,32,2048]{2,1,0:T(8,128)(2,1)}), bf16[8,32,2048]{2,1,0:T(8,128)(2,1)S(1)}, u32[]{:S(2)}, u32[]{:S(2)}) async-start(bf16[8,32,2048]{2,1,0:T(8,128)(2,1)} %bitcast.50), calls=%async_computation.4 | async-start | bytes 2097152 | tf_op jit(solution)/shard_map/all_to_all | solution.py:76
Sparse Core Ops, SparseCore 0:
  11.4 175.1 all-gather.2
  224.5 265.3 reduce-scatter.4
  496.4 264.6 reduce-scatter.2
